TPU v7x, 32 devices: a whole 2x2x4 slice. The times are simulated.
32 devices in a mesh: energy: 16 (over z, y, x), space: 2 (over core).
Axes of the slice: x: 2, y: 2, z: 4, core: 2. Of those that a mesh axis runs over, the one named last changes fastest.
Arguments:
- green0: bfloat16 [128, 2, 2, 192, 192], P('energy', 'space'), may hold values from -1.5 to 1
- coupling: bfloat16 [2, 192, 192], P('space'), may hold values from -0.375 to 0.375
- pattern: int32 [2, 4, 4], P('space'), may hold values 0 or 1
- broaden: bfloat16 [128, 2, 192, 192], P('energy', 'space'), may hold values from -0.5 to 1.5
- screened: float32 [128, 2, 192, 384], P(None, 'space', 'energy'), may hold values from -6 to 6
- order: int32 [192], replicated, may hold values from 0 to 191, each once
Outputs:
- sigma: float32 [128, 2, 192, 384], P('energy', 'space')
All inputs are finite; a program needn't handle non-finite values. No bound on the sum of `pattern` on one device may be relied on, other than what follows from the above.
Results may differ from a plain program's by a relative error of at most 0.0059.
Values may be sent and summed in bfloat16 or wider, within the bound.
A program may use at most 128 MiB of HBM per device.

v0:
```python
import functools
import math

import jax
import jax.numpy as jnp
import numpy as np
from jax import lax
from jax.experimental import pallas as pl
from jax.experimental.pallas import tpu as pltpu
from jax.sharding import PartitionSpec as P

F32 = jnp.float32
BF16 = jnp.bfloat16
PLAIN = ((1,), (0,))
LAST = ((1,), (1,))
FIRST = ((0,), (0,))


def dot(a, b, dims=PLAIN):
    return lax.dot_general(a, b, (dims, ((), ())), preferred_element_type=F32)


def complex_dot(left, right_re, right_im, dims=PLAIN):
    rows = left.shape[0] // 2
    with_re = dot(left, right_re, dims)
    with_im = dot(left, right_im, dims)
    return (with_re[:rows] - with_im[rows:], with_im[:rows] + with_re[rows:])


def stack(pair):
    return jnp.concatenate(pair, axis=0)


def born_kernel(first_ref, pattern_ref, green_ref, coupling_ref, send_ref, mult_ref, base_ref, couple_s):
    many, both, size = green_ref.shape
    rows = both // 2
    batch = range(many)

    @pl.when(pl.program_id(0) == 0)
    def _():
        tiles = pattern_ref.shape[0]
        tile_size = size // tiles
        lane = lax.broadcasted_iota(jnp.int32, (tile_size, size), 1)
        for i in range(tiles):
            keep = jnp.zeros((tile_size, size), F32)
            for j in range(tiles):
                inside = (lane >= j * tile_size) & (lane < (j + 1) * tile_size)
                keep = jnp.where(inside, pattern_ref[i, j].astype(F32), keep)
            at = slice(i * tile_size, (i + 1) * tile_size)
            couple_s[at, :] = (coupling_ref[at, :].astype(F32) * keep).astype(BF16)

    couple = couple_s[...]
    green = [green_ref[i] for i in batch]
    factor = [dot(g, couple).astype(BF16) for g in green]

    @pl.when(first_ref[0] == 1)
    def _():
        moved = [
            stack(complex_dot(f, g[:rows], g[rows:])).astype(BF16) for f, g in zip(factor, green)
        ]
        for i in batch:
            re, im = complex_dot(moved[i], factor[i][:rows], factor[i][rows:], LAST)
            re = green[i][:rows].astype(F32) + re
            im = green[i][rows:].astype(F32) + im
            base_ref[i, :rows] = re
            base_ref[i, rows:] = im
            send_ref[i] = jnp.concatenate([re, im], axis=1).astype(BF16)
            mult_ref[i] = green[i]

    @pl.when(first_ref[0] == 0)
    def _():
        for i in batch:
            base_ref[i] = green[i].astype(F32)
            added = [dot(factor[i][:rows], couple, FIRST), dot(factor[i][rows:], couple, FIRST)]
            send_ref[i] = jnp.concatenate(added, axis=1).astype(BF16)
            mult_ref[i] = factor[i]


def lesser_kernel(
    owners, first_ref, mult_ref, got_ref, base_ref, gamma_ref, pick_ref, mix_ref, out_ref, full_s, slots_s
):
    step = pl.program_id(0)
    many, both, size = mult_ref.shape
    rows = both // 2
    batch = range(many)
    mult = [mult_ref[i] for i in batch]
    moved = [
        stack(complex_dot(mult[i], got_ref[i, :, :rows], got_ref[i, :, rows:])).astype(BF16)
        for i in batch
    ]

    def finish(dims):
        for i in batch:
            extra = stack(complex_dot(moved[i], mult[i][:rows], mult[i][rows:], dims))
            full_s[i] = (base_ref[i] + extra).astype(BF16)

    @pl.when(first_ref[0] == 1)
    def _():
        finish(PLAIN)

    @pl.when(first_ref[0] == 0)
    def _():
        finish(LAST)

    full = [full_s[i] for i in batch]
    pick = pick_ref[...]
    weighted = [dot(full[i], gamma_ref[i]).astype(BF16) for i in batch]
    weighted = [stack((dot(pick, w[:rows]), dot(pick, w[rows:]))).astype(BF16) for w in weighted]
    share = rows // owners
    for i in batch:
        with_re = dot(weighted[i], full[i][:rows], LAST)
        with_im = dot(weighted[i], full[i][rows:], LAST)
        lesser = jnp.concatenate(
            [with_im[:rows] - with_re[rows:], with_re[:rows] + with_im[rows:]], axis=1
        ).astype(BF16)
        at = pl.ds(pl.multiple_of((step * many + i) * owners, owners), owners)
        for r in range(share):
            slots_s[r, at, :] = lesser[r * owners : (r + 1) * owners]

    @pl.when(step == pl.num_programs(0) - 1)
    def _():
        mix = mix_ref[...]
        width = 2 * size
        for r in range(share):
            out_ref[:, r * width : (r + 1) * width] = dot(mix, slots_s[r]).astype(BF16)


def times_i(values):
    half = values.shape[1] // 2
    return jnp.concatenate([-values[:, half:], values[:, :half]], axis=1)


def transform(table, upper, lower):
    both = dot(table, jnp.concatenate([upper, lower], axis=0).astype(BF16))
    points = upper.shape[0]
    return both[:points] + both[points:]


def exchange_kernel(
    owners,
    groups,
    scale,
    table_ref,
    mixed_ref,
    screened_ref,
    back_ref,
    screened_s,
    spectrum_s,
    got_s,
    sigma_s,
    away_sent,
    away_landed,
    back_sent,
    back_landed,
    own_sem,
):
    me = lax.axis_index("energy")
    points, share, width = screened_s.shape
    each = share // groups
    span = each * width

    def columns(g):
        return pl.ds(g * span, span)

    def away(g, k):
        peer = lax.rem(me + k, owners)
        return pltpu.make_async_remote_copy(
            src_ref=mixed_ref.at[peer, :, columns(g)],
            dst_ref=got_s.at[me, :, columns(g)],
            send_sem=away_sent.at[g, k - 1],
            recv_sem=away_landed.at[g, k - 1],
            device_id={"energy": peer},
            device_id_type=pl.DeviceIdType.MESH,
        )

    def back(g, k):
        peer = lax.rem(me + k, owners)
        return pltpu.make_async_remote_copy(
            src_ref=sigma_s.at[peer, :, columns(g)],
            dst_ref=back_ref.at[me, :, columns(g)],
            send_sem=back_sent.at[g, k - 1],
            recv_sem=back_landed.at[g, k - 1],
            device_id={"energy": peer},
            device_id_type=pl.DeviceIdType.MESH,
        )

    def for_peers(action):
        lax.fori_loop(1, owners, lambda k, c: (action(k), c)[1], 0)

    barrier = pltpu.get_barrier_semaphore()
    for_peers(
        lambda k: pl.semaphore_signal(
            barrier,
            inc=1,
            device_id={"energy": lax.rem(me + k, owners)},
            device_id_type=pl.DeviceIdType.MESH,
        )
    )
    load = pltpu.make_async_copy(screened_ref, screened_s, own_sem.at[0])
    load.start()
    keep = pltpu.make_async_copy(mixed_ref.at[me], got_s.at[me], own_sem.at[1])
    keep.start()
    pl.semaphore_wait(barrier, owners - 1)
    for g in range(groups):
        for_peers(lambda k: away(g, k).start())
    load.wait()
    table = table_ref[...]
    for r in range(share):
        values = screened_s[:, r, :]
        spectrum_s[:, r * width : (r + 1) * width] = transform(table, values, times_i(values)) * scale
    keep.wait()
    half = width // 2
    owns = []
    for g in range(groups):
        for_peers(lambda k: away(g, k).wait_recv())
        for r in range(g * each, (g + 1) * each):
            at = slice(r * width, (r + 1) * width)
            values = got_s[:, :, at].astype(F32).reshape(points, width)
            kernel = spectrum_s[:, at]
            spectrum = transform(table, values, times_i(values))
            kernel_re = jnp.concatenate([kernel[:, :half], kernel[:, :half]], axis=1)
            kernel_im = jnp.concatenate([kernel[:, half:], kernel[:, half:]], axis=1)
            product = spectrum * kernel_re + times_i(spectrum) * kernel_im
            result = transform(table, times_i(product), product)
            sigma_s[:, :, at] = result.reshape(owners, points // owners, width).astype(BF16)
        for_peers(lambda k: back(g, k).start())
        own = pltpu.make_async_copy(
            sigma_s.at[me, :, columns(g)], back_ref.at[me, :, columns(g)], own_sem.at[2 + g]
        )
        own.start()
        owns.append(own)
    for g in range(groups):
        owns[g].wait()
        for_peers(lambda k: away(g, k).wait_send())
        for_peers(lambda k: back(g, k).wait())


def restore_kernel(owners, values_ref, unmix_ref, place_ref, out_ref, slots_s):
    step = pl.program_id(0)
    many, size, width = out_ref.shape
    share = size // owners

    @pl.when(step == 0)
    def _():
        unmix = unmix_ref[...]
        for r in range(share):
            slots_s[r] = dot(unmix, values_ref[:, r * width : (r + 1) * width]).astype(BF16)

    for i in range(many):
        at = pl.ds(pl.multiple_of((step * many + i) * owners, owners), owners)
        ordered = jnp.concatenate([slots_s[r, at, :] for r in range(share)], axis=0)
        out_ref[i] = dot(place_ref[...], ordered)


def whole(shape):
    return pl.BlockSpec(shape, lambda e: (0,) * len(shape))


def energies(many, *shape):
    return pl.BlockSpec((many,) + shape, lambda e: (e,) + (0,) * len(shape))


def params():
    return pltpu.CompilerParams(dimension_semantics=("arbitrary",))


def cost(flops, moved):
    return pl.CostEstimate(flops=int(flops), bytes_accessed=int(moved), transcendentals=0)


def on_device(owners, green0, coupling, pattern, broaden, screened, order):
    here = green0.shape[0]
    size = green0.shape[-1]
    points = screened.shape[0]
    share = size // owners
    width = 2 * size
    flat = share * width
    green = green0.reshape(here, 2 * size, size)
    gamma = broaden.reshape(here, size, size)
    many = max(count for count in (1, 2, 4) if here % count == 0)
    first = (lax.axis_index("space") == 0).astype(jnp.int32).reshape(1)
    by_row = order.reshape(owners, share).T.reshape(-1)
    ids = jnp.arange(size, dtype=jnp.int32)
    pick = (by_row[:, None] == ids[None, :]).astype(BF16)
    place = (by_row[None, :] == ids[:, None]).astype(BF16)

    ticks = np.arange(points)
    angles = (ticks[:, None] * ticks[None, :] % points) * (2.0 * math.pi / points)
    exact = np.concatenate([np.cos(angles), -np.sin(angles)], axis=1)
    high = exact.astype(BF16)
    low = (exact - high.astype(np.float64)).astype(BF16)
    table = jnp.asarray(np.concatenate([high, low], axis=0))
    where = np.arange(here * owners)
    source = (where % here) * owners + where // here
    mix_np = (source[:, None] == where[None, :]).astype(np.float32)
    mix = jnp.asarray(mix_np.astype(BF16))
    unmix = jnp.asarray(mix_np.T.astype(BF16))

    smem = pl.BlockSpec(memory_space=pltpu.SMEM)
    cell = (2 * size, size)
    work = 2.0 * here * size**3
    send, mult, base = pl.pallas_call(
        born_kernel,
        grid=(here // many,),
        in_specs=[smem, smem, energies(many, *cell), whole((size, size))],
        out_specs=[energies(many, size, width), energies(many, *cell), energies(many, *cell)],
        out_shape=[
            jax.ShapeDtypeStruct((here, size, width), BF16),
            jax.ShapeDtypeStruct((here,) + cell, BF16),
            jax.ShapeDtypeStruct((here,) + cell, F32),
        ],
        scratch_shapes=[pltpu.VMEM((size, size), BF16)],
        compiler_params=params(),
        cost_estimate=cost(10 * work, 10 * here * 2 * size * size),
        name="born",
    )(first, pattern[0], green, coupling[0])
    got = lax.ppermute(send, "space", [(0, 1), (1, 0)])
    mixed = pl.pallas_call(
        functools.partial(lesser_kernel, owners),
        grid=(here // many,),
        in_specs=[
            smem,
            energies(many, *cell),
            energies(many, size, width),
            energies(many, *cell),
            energies(many, size, size),
            whole((size, size)),
            whole((here * owners, here * owners)),
        ],
        out_specs=whole((here * owners, flat)),
        out_shape=jax.ShapeDtypeStruct((here * owners, flat), BF16),
        scratch_shapes=[
            pltpu.VMEM((many,) + cell, BF16),
            pltpu.VMEM((share, here * owners, width), BF16),
        ],
        compiler_params=params(),
        cost_estimate=cost(16 * work, 14 * here * 2 * size * size),
        name="lesser",
    )(first, mult, got, base, gamma, pick, mix)
    groups = max(parts for parts in range(1, 5) if share % parts == 0)
    anywhere = pl.BlockSpec(memory_space=pl.ANY)
    each_way = pltpu.SemaphoreType.DMA((groups, owners - 1))
    returned = pl.pallas_call(
        functools.partial(exchange_kernel, owners, groups, 1.0 / (points * math.sqrt(points))),
        in_specs=[pl.BlockSpec(memory_space=pltpu.VMEM), anywhere, anywhere],
        out_specs=anywhere,
        out_shape=jax.ShapeDtypeStruct((owners, here, flat), BF16),
        scratch_shapes=[
            pltpu.VMEM((points, share, width), F32),
            pltpu.VMEM((points, flat), F32),
            pltpu.VMEM((owners, here, flat), BF16),
            pltpu.VMEM((owners, here, flat), BF16),
            each_way,
            each_way,
            each_way,
            each_way,
            pltpu.SemaphoreType.DMA((2 + groups,)),
        ],
        compiler_params=pltpu.CompilerParams(collective_id=0, has_side_effects=True),
        name="exchange",
    )(table, mixed.reshape(owners, here, flat), screened.reshape(points, share, width))
    returned = returned.reshape(points, flat)
    out = pl.pallas_call(
        functools.partial(restore_kernel, owners),
        grid=(here // many,),
        in_specs=[
            whole((here * owners, flat)),
            whole((here * owners, here * owners)),
            whole((size, size)),
        ],
        out_specs=energies(many, size, width),
        out_shape=jax.ShapeDtypeStruct((here, size, width), F32),
        scratch_shapes=[pltpu.VMEM((share, here * owners, width), BF16)],
        compiler_params=params(),
        cost_estimate=cost(4 * work, 6 * points * flat),
        name="restore",
    )(returned, unmix, place)
    return out[:, None]


def solution(mesh):
    return jax.shard_map(
        functools.partial(on_device, mesh.shape["energy"]),
        mesh=mesh,
        in_specs=(
            P("energy", "space", None, None, None),
            P("space", None, None),
            P("space", None, None),
            P("energy", "space", None, None),
            P(None, "space", "energy", None),
            P(),
        ),
        out_specs=P("energy", "space", None, None),
        check_vma=False,
    )
```

profile of v0, /device:TPU:0, one launch (start us, length us, event | category | flops | bytes accessed | tf_op | source)
XLA Modules:
  0.0 81.9 jit_solution(13896586459436259818)
XLA Ops:
  0.0 0.0 copy-start.2
  0.0 0.0 copy-start
  0.0 5.9 %born.1 = (bf16[8,192,384]{2,1,0:T(8,128)(2,1)}, bf16[8,384,192]{2,1,0:T(8,128)(2,1)}, f32[8,384,192]{2,1,0:T(8,128)}) custom-call(s32[1]{0:T(128)} %bitcast.first_ref, s32[4,4]{1,0:T(4,128)} %bitcast.22, bf16[8,384,192]{2,1,0:T(8,128)(2,1)} %bitcast.20, bf16[192,192]{1,0:T(8,128)(2,1)} %bitcast.21), custom_call_target="tpu_custom_call" | custom-call | flops 1132462080 | bytes 5898240 | tf_op jit(solution)/shard_map/born/pallas_call | solution.py:302
  6.0 0.0 collective-permute-start
  6.0 0.0 copy-done.2
  6.0 0.1 reshape.29
  6.0 0.1 copy.14
  6.1 0.1 eq.32
  6.2 0.0 copy-done
  6.2 2.0 %copy.20 = f32[128,1,12,384]{3,2,0,1:T(8,128)} copy(f32[128,1,12,384]{3,1,2,0:T(1,128)S(1)} %copy-done) | data formatting | bytes 4718592 | tf_op jit(solution)/shard_map/reshape | solution.py:361
  8.2 0.7 fusion.1
  8.9 0.1 collective-permute-done.got_ref
  9.0 0.0 copy-start.1
  9.0 1.1 %copy-done.1 = bf16[8,192,384]{2,1,0:T(8,128)(2,1)} copy-done((bf16[8,192,384]{2,1,0:T(8,128)(2,1)}, bf16[8,192,384]{2,1,0:T(8,128)(2,1)S(1)}, u32[]{:S(2)}) %copy-start.1) | copy-done | bytes 1179672
  10.1 8.1 %lesser.1 = bf16[128,4608]{1,0:T(8,128)(2,1)} custom-call(s32[1]{0:T(128)} %bitcast.first_ref, bf16[8,384,192]{2,1,0:T(8,128)(2,1)} %get-tuple-element.8.mult_ref, bf16[8,192,384]{2,1,0:T(8,128)(2,1)} %copy-done.1, f32[8,384,192]{2,1,0:T(8,128)} %get-tuple-element.10.base_ref, bf16[8,192,192]{2,1,0:T(8,128)(2,1)} %bitcast.18, ...), custom_call_target="tpu_custom_call" | custom-call | flops 1811939328 | bytes 8257536 | tf_op jit(solution)/shard_map/lesser/pallas_call | solution.py:318
  18.2 60.2 %exchange.1 = bf16[16,8,4608]{2,1,0:T(8,128)(2,1)} custom-call(bf16[256,256]{1,0:T(8,128)(2,1)} %constant.12.clone.table_ref, bf16[16,8,4608]{2,1,0:T(8,128)(2,1)} %bitcast.17, f32[128,12,384]{2,1,0:T(8,128)} %bitcast.15), custom_call_target="tpu_custom_call" | custom-call | tf_op jit(solution)/shard_map/exchange/pallas_call | solution.py:343
  78.4 3.6 %restore.1 = f32[8,192,384]{2,1,0:T(8,128)} custom-call(bf16[128,4608]{1,0:T(8,128)(2,1)} %bitcast.16, bf16[128,128]{1,0:T(8,128)(2,1)} %constant.14.clone.unmix_ref, bf16[192,192]{1,0:T(8,128)(2,1)} %get-tuple-element.11.place_ref), custom_call_target="tpu_custom_call" | custom-call | flops 452984832 | bytes 3538944 | tf_op jit(solution)/shard_map/restore/pallas_call | solution.py:363
Async XLA Ops:
  0.0 6.0 %copy-start.2 = (s32[192]{0:T(256)S(1)}, s32[192]{0:T(256)}, u32[]{:S(2)}) copy-start(s32[192]{0:T(256)} %param.14) | copy-start | bytes 2308
  0.0 6.2 %copy-start = (f32[128,1,12,384]{3,1,2,0:T(1,128)S(1)}, f32[128,1,12,384]{3,1,2,0:T(1,128)}, u32[]{:S(2)}) copy-start(f32[128,1,12,384]{3,1,2,0:T(1,128)} %param.13) | copy-start | bytes 7077892
  6.0 3.1 %collective-permute-start = (bf16[8,192,384]{2,1,0:T(8,128)(2,1)}, bf16[8,192,384]{2,1,0:T(8,128)(2,1)S(1)}, u32[]{:S(2)}, u32[]{:S(2)}) collective-permute-start(bf16[8,192,384]{2,1,0:T(8,128)(2,1)} %get-tuple-element.9), channel_id=1, source_target_pairs={{0,1},{1,0},{2,3},{3,2},{4,5},{5,4},{6,7},{7,6},{8,9},{9,8},{10,11... | collective-permute-start | bytes 3538952 | tf_op jit(solution)/shard_map/ppermute | solution.py:317
  9.0 1.1 %copy-start.1 = (bf16[8,192,384]{2,1,0:T(8,128)(2,1)}, bf16[8,192,384]{2,1,0:T(8,128)(2,1)S(1)}, u32[]{:S(2)}) copy-start(bf16[8,192,384]{2,1,0:T(8,128)(2,1)S(1)} %collective-permute-done.got_ref) | copy-start | bytes 3538948
where the time goes:
time: 82.2 us; the launch traced here: 81.9 us
  Pallas kernels  77.8 us (95%)
  local copies, waits for them, and re-layouts  3.32 us (4%)
    pallas_call x1, Pallas kernels, on_device(): pl.pallas_call(functools.partial(exchange_kernel, owners, groups, 1.0 / (...  60.2 us
    pallas_call x1, Pallas kernels, on_device(): pl.pallas_call(functools.partial(lesser_kernel, owners), grid=(here // ma...  8.06 us
    pallas_call x1, Pallas kernels, on_device(): pl.pallas_call(born_kernel, grid=(here // many,), in_specs=[smem, smem, e...  5.95 us
    pallas_call x1, Pallas kernels, on_device(): pl.pallas_call(functools.partial(restore_kernel, owners), grid=(here // m...  3.56 us
    reshape x1, local copies, waits for them, and re-layouts, on_device(): screened.reshape(points, share, width)  1.97 us
  transfers between devices with their start and end apart: 1, of which 1 were waited for; matrix products, arithmetic and copies ran while one was open for 4% of the time, Pallas kernels for 0%

commit v1 on v0

v1 whole, which is shorter than its diff:
```python
import functools
import math

import jax
import jax.numpy as jnp
import numpy as np
from jax import lax
from jax.experimental import pallas as pl
from jax.experimental.pallas import tpu as pltpu
from jax.sharding import PartitionSpec as P

F32 = jnp.float32
BF16 = jnp.bfloat16
PLAIN = ((1,), (0,))
LAST = ((1,), (1,))
FIRST = ((0,), (0,))


def dot(a, b, dims=PLAIN):
    return lax.dot_general(a, b, (dims, ((), ())), preferred_element_type=F32)


def complex_dot(left, right_re, right_im, dims=PLAIN):
    rows = left.shape[0] // 2
    with_re = dot(left, right_re, dims)
    with_im = dot(left, right_im, dims)
    return (with_re[:rows] - with_im[rows:], with_im[:rows] + with_re[rows:])


def stack(pair):
    return jnp.concatenate(pair, axis=0)


def times_i(values):
    half = values.shape[1] // 2
    return jnp.concatenate([-values[:, half:], values[:, :half]], axis=1)


def transform(table, upper, lower):
    both = dot(table, jnp.concatenate([upper, lower], axis=0).astype(BF16))
    points = upper.shape[0]
    return both[:points] + both[points:]


def fused_kernel(
    owners,
    pack,
    scale,
    pattern_ref,
    coupling_ref,
    green_ref,
    gamma_ref,
    order_ref,
    sort_ref,
    turn_ref,
    table_ref,
    unmix_ref,
    screened_ref,
    out_ref,
    coupling_s,
    couple_s,
    turned_s,
    green_s,
    gamma_s,
    order_s,
    sort_s,
    turn_s,
    table_s,
    unmix_s,
    screened_s,
    mult_s,
    other_s,
    base_s,
    send_s,
    map_s,
    pick_s,
    place_s,
    mixed_s,
    got_s,
    spectrum_s,
    sigma_s,
    back_s,
    slots_s,
    result_s,
    load_sem,
    green_sem,
    out_sem,
    map_sent,
    map_landed,
    early_sent,
    early_landed,
    late_sent,
    late_landed,
    back_sent,
    back_landed,
    own_early,
    own_late,
    own_back,
):
    me = lax.axis_index("energy")
    cell = lax.axis_index("space")
    here, both, size = green_s.shape
    rows = both // 2
    width = 2 * size
    share = size // owners
    quads = share // pack
    many = 8 // pack
    batches = here // many
    points = owners * here
    early = max(quads - 1, 1)

    def load(n, source, target):
        return pltpu.make_async_copy(source, target, load_sem.at[n])

    def load_green(b):
        at = pl.ds(b * many, many)
        return pltpu.make_async_copy(green_ref.at[at], green_s.at[at], green_sem.at[b])

    loads = [
        load(n, source, target)
        for n, (source, target) in enumerate(
            (
                (coupling_ref, coupling_s),
                (order_ref, order_s),
                (sort_ref, sort_s),
                (gamma_ref, gamma_s),
                (table_ref, table_s),
                (screened_ref, screened_s),
                (turn_ref, turn_s),
                (unmix_ref, unmix_s),
            )
        )
    ]
    coupling_load, order_load, sort_load, gamma_load, table_load, screened_load, turn_load, unmix_load = loads

    def peer_of(k):
        return lax.rem(me + k, owners)

    def remote(source, target, sent, landed, device):
        return pltpu.make_async_remote_copy(
            src_ref=source,
            dst_ref=target,
            send_sem=sent,
            recv_sem=landed,
            device_id=device,
            device_id_type=pl.DeviceIdType.MESH,
        )

    def share_map(b):
        at = pl.ds(b * many, many)
        return remote(send_s.at[at], map_s.at[at], map_sent.at[b], map_landed.at[b], {"space": 1 - cell})

    def away_early(b, k):
        peer = peer_of(k)
        columns = pl.ds(0, early * width)
        return remote(
            mixed_s.at[peer, b, :, columns],
            got_s.at[me, b, :, columns],
            early_sent.at[b, k - 1],
            early_landed.at[b, k - 1],
            {"energy": peer},
        )

    def away_late(k):
        peer = peer_of(k)
        columns = pl.ds(early * width, (quads - early) * width)
        return remote(
            mixed_s.at[peer, :, :, columns],
            got_s.at[me, :, :, columns],
            late_sent.at[k - 1],
            late_landed.at[k - 1],
            {"energy": peer},
        )

    def back(q, k):
        peer = peer_of(k)
        columns = pl.ds(q * pack * width, pack * width)
        return remote(
            sigma_s.at[peer, :, columns],
            back_s.at[me, :, columns],
            back_sent.at[q, k - 1],
            back_landed.at[q, k - 1],
            {"energy": peer},
        )

    def keep_early(b):
        columns = pl.ds(0, early * width)
        return pltpu.make_async_copy(
            mixed_s.at[me, b, :, columns], got_s.at[me, b, :, columns], own_early.at[b]
        )

    def keep_late():
        columns = pl.ds(early * width, (quads - early) * width)
        return pltpu.make_async_copy(
            mixed_s.at[me, :, :, columns], got_s.at[me, :, :, columns], own_late.at[0]
        )

    def keep_back(q):
        columns = pl.ds(q * pack * width, pack * width)
        return pltpu.make_async_copy(
            sigma_s.at[me, :, columns], back_s.at[me, :, columns], own_back.at[q]
        )

    def for_peers(action):
        lax.fori_loop(1, owners, lambda k, c: (action(k), c)[1], 0)

    barrier = pltpu.get_barrier_semaphore()

    def greet(device):
        pl.semaphore_signal(barrier, inc=1, device_id=device, device_id_type=pl.DeviceIdType.MESH)

    coupling_load.start()
    load_green(0).start()
    for_peers(lambda k: greet({"energy": peer_of(k)}))
    greet({"space": 1 - cell})
    for b in range(1, batches):
        load_green(b).start()
    for each in loads[1:]:
        each.start()

    tiles = pattern_ref.shape[0]
    tile_size = size // tiles
    coupling_load.wait()
    lane = lax.broadcasted_iota(jnp.int32, (tile_size, size), 1)
    for i in range(tiles):
        keep = jnp.zeros((tile_size, size), F32)
        for j in range(tiles):
            inside = (lane >= j * tile_size) & (lane < (j + 1) * tile_size)
            keep = jnp.where(inside, pattern_ref[i, j].astype(F32), keep)
        at = slice(i * tile_size, (i + 1) * tile_size)
        couple_s[at, :] = (coupling_s[at, :].astype(F32) * keep).astype(BF16)

    @pl.when(cell == 1)
    def _():
        turned_s[...] = jnp.transpose(couple_s[...].astype(F32)).astype(BF16)

    def born(b):
        load_green(b).wait()
        batch = [b * many + i for i in range(many)]

        @pl.when(cell == 0)
        def _():
            couple = couple_s[...]
            green = [green_s[e] for e in batch]
            factor = [dot(g, couple).astype(BF16) for g in green]
            moved = [
                stack(complex_dot(f, g[:rows], g[rows:])).astype(BF16) for f, g in zip(factor, green)
            ]
            for e, f, g, m in zip(batch, factor, green, moved):
                base = g.astype(F32) + stack(complex_dot(m, f[:rows], f[rows:], LAST))
                base_s[e] = base
                send_s[e] = base.astype(BF16)
                mult_s[e] = g
                other_s[e] = g

        @pl.when(cell == 1)
        def _():
            couple = couple_s[...]
            turned = turned_s[...]
            green = [green_s[e] for e in batch]
            flipped = [
                stack((dot(turned, g[:rows], LAST), dot(turned, g[rows:], LAST))).astype(BF16)
                for g in green
            ]
            for e, f in zip(batch, flipped):
                send_s[e] = dot(f, couple).astype(BF16)
                other_s[e] = f
            for e, g in zip(batch, green):
                mult_s[e] = dot(g, couple).astype(BF16)
                base_s[e] = g.astype(F32)

    def lesser(b):
        batch = [b * many + i for i in range(many)]
        mult = [mult_s[e] for e in batch]
        other = [other_s[e] for e in batch]
        moved = [
            stack(complex_dot(m, map_s[e, :rows], map_s[e, rows:])).astype(BF16)
            for e, m in zip(batch, mult)
        ]
        full = [
            (base_s[e] + stack(complex_dot(m, o[:rows], o[rows:]))).astype(BF16)
            for e, m, o in zip(batch, moved, other)
        ]
        weighted = [dot(f, gamma_s[e]).astype(BF16) for e, f in zip(batch, full)]
        found = [
            (
                dot(w[:rows], stack((f[rows:], f[:rows])), LAST)
                + dot(w[rows:], stack((-f[:rows], f[rows:])), LAST)
            ).astype(BF16)
            for w, f in zip(weighted, full)
        ]
        block = 8 * owners
        for q in range(quads):
            at = slice(q * block, (q + 1) * block)
            mixed = sum(dot(pick_s[i, at], found[i]) for i in range(many))
            mixed_s[:, b, :, q * width : (q + 1) * width] = mixed.reshape(owners, 8, width).astype(BF16)

    born(0)
    pl.semaphore_wait(barrier, owners)
    share_map(0).start()
    if batches > 1:
        born(1)
        share_map(1).start()
    order_load.wait()
    sort_load.wait()
    ids = lax.broadcasted_iota(jnp.int32, (size, size), 0)
    place = jnp.where(ids == order_s[...], 1.0, 0.0).astype(BF16)
    for i in range(many):
        pick_s[i] = dot(sort_s[i], place, LAST).astype(BF16)
    gamma_load.wait()

    for b in range(batches):
        share_map(b).wait_recv()
        lesser(b)
        for_peers(lambda k: away_early(b, k).start())
        keep_early(b).start()
        if b + 2 < batches:
            born(b + 2)
            share_map(b + 2).start()
    if quads > early:
        for_peers(lambda k: away_late(k).start())
        keep_late().start()
    turn_load.wait()
    place_s[...] = dot(place, turn_s[...]).astype(BF16)
    table_load.wait()
    screened_load.wait()
    unmix_load.wait()
    table = table_s[...]
    pieces = width // 128
    for r in range(share):
        values = jnp.concatenate(
            [
                screened_s[pl.ds(r * pieces + c, points, stride=share * pieces), :]
                for c in range(pieces)
            ],
            axis=1,
        )
        spectrum_s[:, r * width : (r + 1) * width] = transform(table, values, times_i(values)) * scale

    half = width // 2
    row_ids = lax.broadcasted_iota(jnp.int32, (points, points * pack), 0)
    column_ids = lax.broadcasted_iota(jnp.int32, (points, points * pack), 1)
    for q in range(quads):
        if q == 0:
            lax.fori_loop(
                0, batches, lambda b, c: (for_peers(lambda k: away_early(b, k).wait_recv()), c)[1], 0
            )
            for b in range(batches):
                keep_early(b).wait()
        if q == early:
            for_peers(lambda k: away_late(k).wait_recv())
            keep_late().wait()
        packed = got_s[:, :, :, q * width : (q + 1) * width].astype(F32)
        packed = packed.reshape(points * pack, width).astype(BF16)
        for r in range(pack):
            if pack == 1:
                values = packed.astype(F32)
            else:
                chosen = jnp.where(column_ids == row_ids * pack + r, 1.0, 0.0).astype(BF16)
                values = dot(chosen, packed)
            at = slice((q * pack + r) * width, (q * pack + r + 1) * width)
            kernel = spectrum_s[:, at]
            spectrum = transform(table, values, times_i(values))
            kernel_re = jnp.concatenate([kernel[:, :half], kernel[:, :half]], axis=1)
            kernel_im = jnp.concatenate([kernel[:, half:], kernel[:, half:]], axis=1)
            product = spectrum * kernel_re + times_i(spectrum) * kernel_im
            found = transform(table, times_i(product), product)
            sigma_s[:, :, at] = found.reshape(owners, here, width).astype(BF16)
        for_peers(lambda k: back(q, k).start())
        keep_back(q).start()

    unmix = unmix_s[...]
    for q in range(quads):
        for_peers(lambda k: back(q, k).wait_recv())
        keep_back(q).wait()
        for r in range(q * pack, (q + 1) * pack):
            values = back_s[:, :, r * width : (r + 1) * width].astype(F32)
            values = values.reshape(points, width).astype(BF16)
            slots_s[r] = dot(unmix, values).astype(BF16)
    outs = []
    for e in range(here):
        at = slice(e * owners, (e + 1) * owners)
        ordered = jnp.concatenate([slots_s[r, at, :] for r in range(share)], axis=0)
        result_s[e] = dot(place_s[...], ordered).astype(BF16)
        out = pltpu.make_async_copy(result_s.at[e], out_ref.at[e], out_sem.at[e])
        out.start()
        outs.append(out)
    for b in range(batches):
        share_map(b).wait_send()
    lax.fori_loop(
        0, batches, lambda b, c: (for_peers(lambda k: away_early(b, k).wait_send()), c)[1], 0
    )
    if quads > early:
        for_peers(lambda k: away_late(k).wait_send())
    for q in range(quads):
        for_peers(lambda k: back(q, k).wait_send())
    for out in outs:
        out.wait()


def on_device(owners, green0, coupling, pattern, broaden, screened, order):
    here = green0.shape[0]
    size = green0.shape[-1]
    points = screened.shape[0]
    share = size // owners
    width = 2 * size
    flat = share * width
    pack = max(p for p in (1, 2, 4) if share % p == 0 and here % (8 // p) == 0)
    quads = share // pack
    many = 8 // pack
    batches = here // many
    early = max(quads - 1, 1)
    green = green0.reshape(here, 2 * size, size)
    gamma = broaden.reshape(here, size, size)

    ticks = np.arange(points)
    angles = (ticks[:, None] * ticks[None, :] % points) * (2.0 * math.pi / points)
    exact = np.concatenate([np.cos(angles), -np.sin(angles)], axis=1)
    high = exact.astype(BF16)
    low = (exact - high.astype(np.float64)).astype(BF16)
    table = jnp.asarray(np.concatenate([high, low], axis=0))
    where = np.arange(points)
    source = (where % owners) * here + where // owners
    unmix = jnp.asarray((source[:, None] == where[None, :]).astype(np.float32).astype(BF16))
    slot = np.arange(size)
    turn = ((slot % owners) * share + slot // owners)[None, :] == slot[:, None]
    turn = jnp.asarray(turn.astype(np.float32).astype(BF16))
    q, o, i, r = np.meshgrid(
        np.arange(quads), np.arange(owners), np.arange(many), np.arange(pack), indexing="ij"
    )
    wanted = (o * share + q * pack + r).reshape(-1)
    owner_of = i.reshape(-1)
    sort = (wanted[None, :, None] == slot[None, None, :]) & (
        owner_of[None, :, None] == np.arange(many)[:, None, None]
    )
    sort = jnp.asarray(sort.astype(np.float32).astype(BF16))

    anywhere = pl.BlockSpec(memory_space=pl.ANY)
    dma = pltpu.SemaphoreType.DMA
    cell = (here, 2 * size, size)
    packed = (owners, batches, 8, quads * width)
    peers = owners - 1
    result = pl.pallas_call(
        functools.partial(fused_kernel, owners, pack, 1.0 / (points * math.sqrt(points))),
        in_specs=[pl.BlockSpec(memory_space=pltpu.SMEM)] + [anywhere] * 9,
        out_specs=anywhere,
        out_shape=jax.ShapeDtypeStruct((here, size, width), BF16),
        scratch_shapes=[
            pltpu.VMEM((size, size), BF16),
            pltpu.VMEM((size, size), BF16),
            pltpu.VMEM((size, size), BF16),
            pltpu.VMEM(cell, BF16),
            pltpu.VMEM((here, size, size), BF16),
            pltpu.VMEM((1, size), jnp.int32),
            pltpu.VMEM(sort.shape, BF16),
            pltpu.VMEM(turn.shape, BF16),
            pltpu.VMEM(table.shape, BF16),
            pltpu.VMEM(unmix.shape, BF16),
            pltpu.VMEM((points * flat // 128, 128), F32),
            pltpu.VMEM(cell, BF16),
            pltpu.VMEM(cell, BF16),
            pltpu.VMEM(cell, F32),
            pltpu.VMEM(cell, BF16),
            pltpu.VMEM(cell, BF16),
            pltpu.VMEM(sort.shape, BF16),
            pltpu.VMEM((size, size), BF16),
            pltpu.VMEM(packed, BF16),
            pltpu.VMEM(packed, BF16),
            pltpu.VMEM((points, flat), F32),
            pltpu.VMEM((owners, here, flat), BF16),
            pltpu.VMEM((owners, here, flat), BF16),
            pltpu.VMEM((share, points, width), BF16),
            pltpu.VMEM((here, size, width), BF16),
            dma((8,)),
            dma((batches,)),
            dma((here,)),
            dma((batches,)),
            dma((batches,)),
            dma((batches, peers)),
            dma((batches, peers)),
            dma((peers,)),
            dma((peers,)),
            dma((quads, peers)),
            dma((quads, peers)),
            dma((batches,)),
            dma((1,)),
            dma((quads,)),
        ],
        compiler_params=pltpu.CompilerParams(collective_id=0, has_side_effects=True),
        name="fused",
    )(
        pattern[0],
        coupling[0],
        green,
        gamma,
        order.reshape(1, size),
        sort,
        turn,
        table,
        unmix,
        screened.reshape(points * flat // 128, 128),
    )
    return result.astype(F32)[:, None]


def solution(mesh):
    return jax.shard_map(
        functools.partial(on_device, mesh.shape["energy"]),
        mesh=mesh,
        in_specs=(
            P("energy", "space", None, None, None),
            P("space", None, None),
            P("space", None, None),
            P("energy", "space", None, None),
            P(None, "space", "energy", None),
            P(),
        ),
        out_specs=P("energy", "space", None, None),
        check_vma=False,
    )
```

time: 82.2 us -> 68.9 us (0.84)
  Pallas kernels: 77.8 us -> 65.6 us
  local copies, waits for them, and re-layouts: 3.32 us -> 0 us
  other arithmetic: 0.73 us -> 2.83 us
    pallas_call x4 -> x1, Pallas kernels: 77.8 us -> 65.6 us  [on_device(): pl.pallas_call(functools.partial(fused_kernel, owners, pack, 1.0 / (point...]
    broadcast_in_dim x0 -> x1, other arithmetic: none -> 2.83 us  [on_device(): return result.astype(F32)[:, None]]
    reshape x2 -> x0, local copies, waits for them, and re-layouts: 2.05 us -> none  [the longest x1 1.97 us: on_device(): screened.reshape(points, share, width)]
    unnamed x6 -> x0, local copies, waits for them, and re-layouts: 1.1 us -> none
  transfers between devices with their start and end apart: 1 -> 0, of which waited for: 1 -> 0; matrix products, arithmetic and copies ran while one was open for 4% -> 0% of each run, Pallas kernels for 0% -> 0%
where the time goes in v1:
time: 68.9 us; the launch traced here: 68.5 us
  Pallas kernels  65.6 us (95%)
  other arithmetic  2.83 us (4%)
    pallas_call x1, Pallas kernels, on_device(): pl.pallas_call(functools.partial(fused_kernel, owners, pack, 1.0 / (point...  65.6 us
    broadcast_in_dim x1, other arithmetic, on_device(): return result.astype(F32)[:, None]  2.83 us

profile of v1, /device:TPU:0, one launch (start us, length us, event | category | flops | bytes accessed | tf_op | source)
XLA Modules:
  0.0 68.5 jit_solution(10174728281192599145)
XLA Ops:
  0.0 65.6 %fused.1 = bf16[8,192,384]{2,1,0:T(8,128)(2,1)} custom-call(s32[4,4]{1,0:T(4,128)} %bitcast.16, bf16[192,192]{1,0:T(8,128)(2,1)} %bitcast.15, bf16[8,384,192]{2,1,0:T(8,128)(2,1)} %bitcast.13, bf16[8,192,192]{2,1,0:T(8,128)(2,1)} %bitcast.14, s32[1,192]{1,0:T(1,128)} %bitcast.17, bf16[2,384,192]{2,1,0:T(8,128)(2,1)} %constant.11.clone.sort_ref, ...), custom_call_target="tpu_custom_call" | custom-call | tf_op jit(solution)/shard_map/fused/pallas_call | solution.py:443
  65.6 2.8 %bitcast_convert_fusion = f32[8,1,192,384]{3,2,1,0:T(8,128)} fusion(bf16[8,192,384]{2,1,0:T(8,128)(2,1)} %fused.1), kind=kLoop, calls=%fused_computation | loop fusion | flops 589824 | bytes 3538944 | tf_op jit(solution)/shard_map/broadcast_in_dim | solution.py:503

commit v2 on v1

--- a/solution.py
+++ b/solution.py
@@ -56,7 +56,9 @@
     table_ref,
     unmix_ref,
     screened_ref,
-    out_ref,
+    slots_s,
+    place_s,
+    pattern_s,
     coupling_s,
     couple_s,
     turned_s,
@@ -74,28 +76,22 @@
     send_s,
     map_s,
     pick_s,
-    place_s,
     mixed_s,
     got_s,
     spectrum_s,
     sigma_s,
     back_s,
-    slots_s,
-    result_s,
     load_sem,
     green_sem,
-    out_sem,
     map_sent,
     map_landed,
-    early_sent,
-    early_landed,
-    late_sent,
-    late_landed,
+    away_sent,
+    away_landed,
     back_sent,
     back_landed,
-    own_early,
-    own_late,
+    own_away,
     own_back,
+    ready_sem,
 ):
     me = lax.axis_index("energy")
     cell = lax.axis_index("space")
@@ -108,6 +104,7 @@
     batches = here // many
     points = owners * here
     early = max(quads - 1, 1)
+    parts = 1 if batches == 1 else 2 if quads == 1 else 3
 
     def load(n, source, target):
         return pltpu.make_async_copy(source, target, load_sem.at[n])
@@ -120,6 +117,7 @@
         load(n, source, target)
         for n, (source, target) in enumerate(
             (
+                (pattern_ref, pattern_s),
                 (coupling_ref, coupling_s),
                 (order_ref, order_s),
                 (sort_ref, sort_s),
@@ -131,7 +129,7 @@
             )
         )
     ]
-    coupling_load, order_load, sort_load, gamma_load, table_load, screened_load, turn_load, unmix_load = loads
+    pattern_load, coupling_load, order_load, sort_load, gamma_load, table_load, screened_load, turn_load, unmix_load = loads
 
     def peer_of(k):
         return lax.rem(me + k, owners)
@@ -150,25 +148,21 @@
         at = pl.ds(b * many, many)
         return remote(send_s.at[at], map_s.at[at], map_sent.at[b], map_landed.at[b], {"space": 1 - cell})
 
-    def away_early(b, k):
+    def piece(part):
+        if part == 0:
+            return pl.ds(0, 1), pl.ds(0, quads * width)
+        if part == 1:
+            return pl.ds(1, batches - 1), pl.ds(0, early * width)
+        return pl.ds(1, batches - 1), pl.ds(early * width, (quads - early) * width)
+
+    def away(part, k):
         peer = peer_of(k)
-        columns = pl.ds(0, early * width)
+        at, columns = piece(part)
         return remote(
-            mixed_s.at[peer, b, :, columns],
-            got_s.at[me, b, :, columns],
-            early_sent.at[b, k - 1],
-            early_landed.at[b, k - 1],
-            {"energy": peer},
-        )
-
-    def away_late(k):
-        peer = peer_of(k)
-        columns = pl.ds(early * width, (quads - early) * width)
-        return remote(
-            mixed_s.at[peer, :, :, columns],
-            got_s.at[me, :, :, columns],
-            late_sent.at[k - 1],
-            late_landed.at[k - 1],
+            mixed_s.at[peer, at, :, columns],
+            got_s.at[me, at, :, columns],
+            away_sent.at[part, k - 1],
+            away_landed.at[part, k - 1],
             {"energy": peer},
         )
 
@@ -183,16 +177,10 @@
             {"energy": peer},
         )
 
-    def keep_early(b):
-        columns = pl.ds(0, early * width)
+    def keep(part):
+        at, columns = piece(part)
         return pltpu.make_async_copy(
-            mixed_s.at[me, b, :, columns], got_s.at[me, b, :, columns], own_early.at[b]
-        )
-
-    def keep_late():
-        columns = pl.ds(early * width, (quads - early) * width)
-        return pltpu.make_async_copy(
-            mixed_s.at[me, :, :, columns], got_s.at[me, :, :, columns], own_late.at[0]
+            mixed_s.at[me, at, :, columns], got_s.at[me, at, :, columns], own_away.at[part]
         )
 
     def keep_back(q):
@@ -205,30 +193,53 @@
         lax.fori_loop(1, owners, lambda k, c: (action(k), c)[1], 0)
 
     barrier = pltpu.get_barrier_semaphore()
+    doubling = owners & (owners - 1) == 0
+    near = [1 << n for n in range(owners.bit_length() - 1)] if doubling else range(1, owners)
+    rounds = len(near) - 1 if doubling else 0
+
+    def peer_at(distance):
+        return jnp.bitwise_xor(me, distance) if doubling else lax.rem(me + distance, owners)
+
+    def pass_on(n):
+        if n < rounds:
+            pl.semaphore_signal(
+                ready_sem.at[n],
+                inc=1,
+                device_id={"energy": peer_at(near[n])},
+                device_id_type=pl.DeviceIdType.MESH,
+            )
+
+    def wait_for_round(n):
+        if n < rounds:
+            pl.semaphore_wait(ready_sem.at[n], 1)
 
     def greet(device):
         pl.semaphore_signal(barrier, inc=1, device_id=device, device_id_type=pl.DeviceIdType.MESH)
 
+    greet({"space": 1 - cell})
+    for distance in near:
+        greet({"energy": peer_at(distance)})
+    pattern_load.start()
     coupling_load.start()
-    load_green(0).start()
-    for_peers(lambda k: greet({"energy": peer_of(k)}))
-    greet({"space": 1 - cell})
-    for b in range(1, batches):
+    for b in range(batches):
         load_green(b).start()
-    for each in loads[1:]:
+    for each in loads[2:]:
         each.start()
-
-    tiles = pattern_ref.shape[0]
+    pl.semaphore_wait(barrier, 1 + len(near))
+    pass_on(0)
+
+    tiles = pattern_s.shape[0]
     tile_size = size // tiles
+    pattern_load.wait()
     coupling_load.wait()
     lane = lax.broadcasted_iota(jnp.int32, (tile_size, size), 1)
     for i in range(tiles):
-        keep = jnp.zeros((tile_size, size), F32)
+        mask = jnp.zeros((tile_size, size), F32)
         for j in range(tiles):
             inside = (lane >= j * tile_size) & (lane < (j + 1) * tile_size)
-            keep = jnp.where(inside, pattern_ref[i, j].astype(F32), keep)
+            mask = jnp.where(inside, pattern_s[i, j].astype(F32), mask)
         at = slice(i * tile_size, (i + 1) * tile_size)
-        couple_s[at, :] = (coupling_s[at, :].astype(F32) * keep).astype(BF16)
+        couple_s[at, :] = (coupling_s[at, :].astype(F32) * mask).astype(BF16)
 
     @pl.when(cell == 1)
     def _():
@@ -296,11 +307,14 @@
             mixed_s[:, b, :, q * width : (q + 1) * width] = mixed.reshape(owners, 8, width).astype(BF16)
 
     born(0)
-    pl.semaphore_wait(barrier, owners)
     share_map(0).start()
+    wait_for_round(0)
+    pass_on(1)
     if batches > 1:
         born(1)
         share_map(1).start()
+    wait_for_round(1)
+    pass_on(2)
     order_load.wait()
     sort_load.wait()
     ids = lax.broadcasted_iota(jnp.int32, (size, size), 0)
@@ -312,14 +326,18 @@
     for b in range(batches):
         share_map(b).wait_recv()
         lesser(b)
-        for_peers(lambda k: away_early(b, k).start())
-        keep_early(b).start()
+        if b == 0:
+            for n in range(2, rounds):
+                wait_for_round(n)
+                pass_on(n + 1)
+            for_peers(lambda k: away(0, k).start())
+            keep(0).start()
         if b + 2 < batches:
             born(b + 2)
             share_map(b + 2).start()
-    if quads > early:
-        for_peers(lambda k: away_late(k).start())
-        keep_late().start()
+    for part in range(1, parts):
+        for_peers(lambda k: away(part, k).start())
+        keep(part).start()
     turn_load.wait()
     place_s[...] = dot(place, turn_s[...]).astype(BF16)
     table_load.wait()
@@ -341,15 +359,10 @@
     row_ids = lax.broadcasted_iota(jnp.int32, (points, points * pack), 0)
     column_ids = lax.broadcasted_iota(jnp.int32, (points, points * pack), 1)
     for q in range(quads):
-        if q == 0:
-            lax.fori_loop(
-                0, batches, lambda b, c: (for_peers(lambda k: away_early(b, k).wait_recv()), c)[1], 0
-            )
-            for b in range(batches):
-                keep_early(b).wait()
-        if q == early:
-            for_peers(lambda k: away_late(k).wait_recv())
-            keep_late().wait()
+        for part in range(parts):
+            if q == (early if part == 2 else 0):
+                for_peers(lambda k: away(part, k).wait_recv())
+                keep(part).wait()
         packed = got_s[:, :, :, q * width : (q + 1) * width].astype(F32)
         packed = packed.reshape(points * pack, width).astype(BF16)
         for r in range(pack):
@@ -377,23 +390,27 @@
             values = back_s[:, :, r * width : (r + 1) * width].astype(F32)
             values = values.reshape(points, width).astype(BF16)
             slots_s[r] = dot(unmix, values).astype(BF16)
+    for b in range(batches):
+        share_map(b).wait_send()
+    for part in range(parts):
+        for_peers(lambda k: away(part, k).wait_send())
+    for q in range(quads):
+        for_peers(lambda k: back(q, k).wait_send())
+
+
+def restore_kernel(slots_ref, place_ref, out_ref, result_s, out_sem):
+    here, size, width = result_s.shape
+    share, points, _ = slots_ref.shape
+    owners = points // here
+    place = place_ref[...]
     outs = []
     for e in range(here):
         at = slice(e * owners, (e + 1) * owners)
-        ordered = jnp.concatenate([slots_s[r, at, :] for r in range(share)], axis=0)
-        result_s[e] = dot(place_s[...], ordered).astype(BF16)
+        ordered = jnp.concatenate([slots_ref[r, at, :] for r in range(share)], axis=0)
+        result_s[e] = dot(place, ordered)
         out = pltpu.make_async_copy(result_s.at[e], out_ref.at[e], out_sem.at[e])
         out.start()
         outs.append(out)
-    for b in range(batches):
-        share_map(b).wait_send()
-    lax.fori_loop(
-        0, batches, lambda b, c: (for_peers(lambda k: away_early(b, k).wait_send()), c)[1], 0
-    )
-    if quads > early:
-        for_peers(lambda k: away_late(k).wait_send())
-    for q in range(quads):
-        for_peers(lambda k: back(q, k).wait_send())
     for out in outs:
         out.wait()
 
@@ -435,17 +452,22 @@
     )
     sort = jnp.asarray(sort.astype(np.float32).astype(BF16))
 
-    anywhere = pl.BlockSpec(memory_space=pl.ANY)
+    anywhere = pl.BlockSpec(memory_space=pltpu.HBM)
     dma = pltpu.SemaphoreType.DMA
     cell = (here, 2 * size, size)
     packed = (owners, batches, 8, quads * width)
     peers = owners - 1
-    result = pl.pallas_call(
+    vmem = pl.BlockSpec(memory_space=pltpu.VMEM)
+    slots, place = pl.pallas_call(
         functools.partial(fused_kernel, owners, pack, 1.0 / (points * math.sqrt(points))),
-        in_specs=[pl.BlockSpec(memory_space=pltpu.SMEM)] + [anywhere] * 9,
-        out_specs=anywhere,
-        out_shape=jax.ShapeDtypeStruct((here, size, width), BF16),
+        in_specs=[anywhere] * 10,
+        out_specs=[vmem, vmem],
+        out_shape=[
+            jax.ShapeDtypeStruct((share, points, width), BF16),
+            jax.ShapeDtypeStruct((size, size), BF16),
+        ],
         scratch_shapes=[
+            pltpu.SMEM(pattern.shape[1:], jnp.int32),
             pltpu.VMEM((size, size), BF16),
             pltpu.VMEM((size, size), BF16),
             pltpu.VMEM((size, size), BF16),
@@ -463,32 +485,28 @@
             pltpu.VMEM(cell, BF16),
             pltpu.VMEM(cell, BF16),
             pltpu.VMEM(sort.shape, BF16),
-            pltpu.VMEM((size, size), BF16),
             pltpu.VMEM(packed, BF16),
             pltpu.VMEM(packed, BF16),
             pltpu.VMEM((points, flat), F32),
             pltpu.VMEM((owners, here, flat), BF16),
             pltpu.VMEM((owners, here, flat), BF16),
-            pltpu.VMEM((share, points, width), BF16),
-            pltpu.VMEM((here, size, width), BF16),
-            dma((8,)),
-            dma((batches,)),
-            dma((here,)),
+            dma((9,)),
             dma((batches,)),
             dma((batches,)),
-            dma((batches, peers)),
-            dma((batches, peers)),
-            dma((peers,)),
-            dma((peers,)),
+            dma((batches,)),
+            dma((3, peers)),
+            dma((3, peers)),
             dma((quads, peers)),
             dma((quads, peers)),
-            dma((batches,)),
-            dma((1,)),
+            dma((3,)),
             dma((quads,)),
+            pltpu.SemaphoreType.REGULAR((owners.bit_length(),)),
         ],
-        compiler_params=pltpu.CompilerParams(collective_id=0, has_side_effects=True),
+        compiler_params=pltpu.CompilerParams(
+            collective_id=0, has_side_effects=True, vmem_limit_bytes=56 << 20
+        ),
         name="fused",
-    )(
+    )(*(pltpu.with_memory_space_constraint(value, pltpu.HBM) for value in (
         pattern[0],
         coupling[0],
         green,
@@ -499,8 +517,17 @@
         table,
         unmix,
         screened.reshape(points * flat // 128, 128),
-    )
-    return result.astype(F32)[:, None]
+    )))
+    result = pl.pallas_call(
+        restore_kernel,
+        in_specs=[vmem, vmem],
+        out_specs=anywhere,
+        out_shape=jax.ShapeDtypeStruct((here, size, width), F32),
+        scratch_shapes=[pltpu.VMEM((here, size, width), F32), dma((here,))],
+        compiler_params=pltpu.CompilerParams(vmem_limit_bytes=16 << 20),
+        name="restore",
+    )(slots, place)
+    return result[:, None]
 
 
 def solution(mesh):

time: 68.9 us -> 68 us (0.987)
  other arithmetic: 2.83 us -> 0 us
  local copies, waits for them, and re-layouts: 0 us -> 2.16 us
    broadcast_in_dim x1 -> x0, other arithmetic: 2.83 us -> none  [on_device(): return result.astype(F32)[:, None]]
    pallas_call x1, Pallas kernels: 65.6 us -> 63.4 us  [on_device(): pl.pallas_call(functools.partial(fused_kernel, owners, pack, 1.0 / (point...]
    unnamed x0 -> x4, local copies, waits for them, and re-layouts: none -> 2.16 us
    pallas_call x0 -> x1, Pallas kernels: none -> 1.67 us  [on_device(): pl.pallas_call(restore_kernel, in_specs=[vmem, vmem], out_specs=anywhere,...]
where the time goes in v2:
time: 68 us; the launch traced here: 67.4 us
  Pallas kernels  65.1 us (96%)
  local copies, waits for them, and re-layouts  2.16 us (3%)
    pallas_call x1, Pallas kernels, on_device(): pl.pallas_call(functools.partial(fused_kernel, owners, pack, 1.0 / (point...  63.4 us
    unnamed x4, local copies, waits for them, and re-layouts  2.16 us
    pallas_call x1, Pallas kernels, on_device(): pl.pallas_call(restore_kernel, in_specs=[vmem, vmem], out_specs=anywhere,...  1.67 us

profile of v2, /device:TPU:0, one launch (start us, length us, event | category | flops | bytes accessed | tf_op | source)
XLA Modules:
  0.0 67.4 jit_solution(15213430354127152817)
XLA Ops:
  0.0 63.4 %fused.1 = (bf16[12,128,384]{2,1,0:T(8,128)(2,1)}, bf16[192,192]{1,0:T(8,128)(2,1)}) custom-call(s32[4,4]{1,0:T(4,128)} %bitcast.13, bf16[192,192]{1,0:T(8,128)(2,1)} %bitcast.12, bf16[8,384,192]{2,1,0:T(8,128)(2,1)} %bitcast.10, bf16[8,192,192]{2,1,0:T(8,128)(2,1)} %bitcast.11, s32[1,192]{1,0:T(1,128)} %bitcast.14, ...), custom_call_target="tpu_custom_call" | custom-call | tf_op jit(solution)/shard_map/fused/pallas_call | solution.py:461
  63.4 0.0 copy-start
  63.5 1.3 %copy-done = bf16[12,128,384]{2,1,0:T(8,128)(2,1)S(1)} copy-done((bf16[12,128,384]{2,1,0:T(8,128)(2,1)S(1)}, bf16[12,128,384]{2,1,0:T(8,128)(2,1)}, u32[]{:S(2)}) %copy-start) | copy-done | bytes 1179672
  64.7 0.0 copy-start.1
  64.7 0.9 %copy-done.1 = bf16[192,192]{1,0:T(8,128)(2,1)S(1)} copy-done((bf16[192,192]{1,0:T(8,128)(2,1)S(1)}, bf16[192,192]{1,0:T(8,128)(2,1)}, u32[]{:S(2)}) %copy-start.1) | copy-done | bytes 73752
  65.6 1.7 %restore.1 = f32[8,192,384]{2,1,0:T(8,128)} custom-call(bf16[12,128,384]{2,1,0:T(8,128)(2,1)S(1)} %copy-done, bf16[192,192]{1,0:T(8,128)(2,1)S(1)} %copy-done.1), custom_call_target="tpu_custom_call" | custom-call | tf_op jit(solution)/shard_map/restore/pallas_call | solution.py:521
Async XLA Ops:
  63.4 1.3 %copy-start = (bf16[12,128,384]{2,1,0:T(8,128)(2,1)S(1)}, bf16[12,128,384]{2,1,0:T(8,128)(2,1)}, u32[]{:S(2)}) copy-start(bf16[12,128,384]{2,1,0:T(8,128)(2,1)} %get-tuple-element.7.slots_ref) | copy-start | bytes 3538948
  64.7 0.9 %copy-start.1 = (bf16[192,192]{1,0:T(8,128)(2,1)S(1)}, bf16[192,192]{1,0:T(8,128)(2,1)}, u32[]{:S(2)}) copy-start(bf16[192,192]{1,0:T(8,128)(2,1)} %get-tuple-element.8.place_ref) | copy-start | bytes 221188

commit v3 on v2

--- a/solution.py
+++ b/solution.py
@@ -131,8 +131,14 @@
     ]
     pattern_load, coupling_load, order_load, sort_load, gamma_load, table_load, screened_load, turn_load, unmix_load = loads
 
+    doubling = owners & (owners - 1) == 0
+    low = 1 << (owners.bit_length() - 1) // 2 if doubling else 1
+
     def peer_of(k):
         return lax.rem(me + k, owners)
+
+    def partner_of(k):
+        return jnp.bitwise_xor(me, k) if doubling else peer_of(k)
 
     def remote(source, target, sent, landed, device):
         return pltpu.make_async_remote_copy(
@@ -156,7 +162,7 @@
         return pl.ds(1, batches - 1), pl.ds(early * width, (quads - early) * width)
 
     def away(part, k):
-        peer = peer_of(k)
+        peer = peer_of(k) if part else partner_of(k)
         at, columns = piece(part)
         return remote(
             mixed_s.at[peer, at, :, columns],
@@ -193,40 +199,35 @@
         lax.fori_loop(1, owners, lambda k, c: (action(k), c)[1], 0)
 
     barrier = pltpu.get_barrier_semaphore()
-    doubling = owners & (owners - 1) == 0
-    near = [1 << n for n in range(owners.bit_length() - 1)] if doubling else range(1, owners)
-    rounds = len(near) - 1 if doubling else 0
-
-    def peer_at(distance):
-        return jnp.bitwise_xor(me, distance) if doubling else lax.rem(me + distance, owners)
-
-    def pass_on(n):
-        if n < rounds:
-            pl.semaphore_signal(
-                ready_sem.at[n],
-                inc=1,
-                device_id={"energy": peer_at(near[n])},
-                device_id_type=pl.DeviceIdType.MESH,
-            )
-
-    def wait_for_round(n):
-        if n < rounds:
-            pl.semaphore_wait(ready_sem.at[n], 1)
+    near = list(range(1, low)) + list(range(low, owners, low))
 
     def greet(device):
         pl.semaphore_signal(barrier, inc=1, device_id=device, device_id_type=pl.DeviceIdType.MESH)
 
+    def say_ready(d):
+        pl.semaphore_signal(
+            ready_sem.at[d],
+            inc=1,
+            device_id={"energy": partner_of(d)},
+            device_id_type=pl.DeviceIdType.MESH,
+        )
+
+    def first_away(d):
+        if d:
+            pl.semaphore_wait(ready_sem.at[d], 1)
+        lax.fori_loop(
+            0 if d else 1, owners // low, lambda j, c: (away(0, d + low * j).start(), c)[1], 0
+        )
+
     greet({"space": 1 - cell})
     for distance in near:
-        greet({"energy": peer_at(distance)})
+        greet({"energy": partner_of(distance)})
     pattern_load.start()
     coupling_load.start()
-    for b in range(batches):
+    for b in range(min(2, batches)):
         load_green(b).start()
-    for each in loads[2:]:
+    for each in (order_load, sort_load, gamma_load):
         each.start()
-    pl.semaphore_wait(barrier, 1 + len(near))
-    pass_on(0)
 
     tiles = pattern_s.shape[0]
     tile_size = size // tiles
@@ -307,14 +308,17 @@
             mixed_s[:, b, :, q * width : (q + 1) * width] = mixed.reshape(owners, 8, width).astype(BF16)
 
     born(0)
+    pl.semaphore_wait(barrier, 1 + len(near))
     share_map(0).start()
-    wait_for_round(0)
-    pass_on(1)
+    for d in range(1, low):
+        say_ready(d)
+    for b in range(2, batches):
+        load_green(b).start()
+    for each in (screened_load, table_load, turn_load, unmix_load):
+        each.start()
     if batches > 1:
         born(1)
         share_map(1).start()
-    wait_for_round(1)
-    pass_on(2)
     order_load.wait()
     sort_load.wait()
     ids = lax.broadcasted_iota(jnp.int32, (size, size), 0)
@@ -327,10 +331,8 @@
         share_map(b).wait_recv()
         lesser(b)
         if b == 0:
-            for n in range(2, rounds):
-                wait_for_round(n)
-                pass_on(n + 1)
-            for_peers(lambda k: away(0, k).start())
+            for d in range(low):
+                first_away(d)
             keep(0).start()
         if b + 2 < batches:
             born(b + 2)
@@ -503,7 +505,7 @@
             pltpu.SemaphoreType.REGULAR((owners.bit_length(),)),
         ],
         compiler_params=pltpu.CompilerParams(
-            collective_id=0, has_side_effects=True, vmem_limit_bytes=56 << 20
+            collective_id=0, has_side_effects=True, vmem_limit_bytes=44 << 20
         ),
         name="fused",
     )(*(pltpu.with_memory_space_constraint(value, pltpu.HBM) for value in (

time: 68 us -> 64.2 us (0.944)
  local copies, waits for them, and re-layouts: 2.16 us -> 0 us
  Pallas kernels: 65.1 us -> 63.8 us
    unnamed x4 -> x0, local copies, waits for them, and re-layouts: 2.16 us -> none
    pallas_call x1, Pallas kernels: 63.4 us -> 62.2 us  [on_device(): pl.pallas_call(functools.partial(fused_kernel, owners, pack, 1.0 / (point...]
where the time goes in v3:
time: 64.2 us; the launch traced here: 64 us
  Pallas kernels  63.8 us (99%)
    pallas_call x1, Pallas kernels, on_device(): pl.pallas_call(functools.partial(fused_kernel, owners, pack, 1.0 / (point...  62.2 us
    pallas_call x1, Pallas kernels, on_device(): pl.pallas_call(restore_kernel, in_specs=[vmem, vmem], out_specs=anywhere,...  1.67 us

profile of v3, /device:TPU:0, one launch (start us, length us, event | category | flops | bytes accessed | tf_op | source)
XLA Modules:
  0.0 64.0 jit_solution(4028103791586194265)
XLA Ops:
  0.0 62.2 %fused.1 = (bf16[12,128,384]{2,1,0:T(8,128)(2,1)S(1)}, bf16[192,192]{1,0:T(8,128)(2,1)S(1)}) custom-call(s32[4,4]{1,0:T(4,128)} %bitcast.13, bf16[192,192]{1,0:T(8,128)(2,1)} %bitcast.12, bf16[8,384,192]{2,1,0:T(8,128)(2,1)} %bitcast.10, bf16[8,192,192]{2,1,0:T(8,128)(2,1)} %bitcast.11, s32[1,192]{1,0:T(1,128)} %bitcast.14, ...), custom_call_target="tpu_custom_call" | custom-call | tf_op jit(solution)/shard_map/fused/pallas_call | solution.py:463
  62.2 1.7 %restore.1 = f32[8,192,384]{2,1,0:T(8,128)} custom-call(bf16[12,128,384]{2,1,0:T(8,128)(2,1)S(1)} %get-tuple-element.7.slots_ref, bf16[192,192]{1,0:T(8,128)(2,1)S(1)} %get-tuple-element.8.place_ref), custom_call_target="tpu_custom_call" | custom-call | tf_op jit(solution)/shard_map/restore/pallas_call | solution.py:523

commit v4 on v3

--- a/solution.py
+++ b/solution.py
@@ -89,8 +89,6 @@
     away_landed,
     back_sent,
     back_landed,
-    own_away,
-    own_back,
     ready_sem,
 ):
     me = lax.axis_index("energy")
@@ -167,8 +165,8 @@
         return remote(
             mixed_s.at[peer, at, :, columns],
             got_s.at[me, at, :, columns],
-            away_sent.at[part, k - 1],
-            away_landed.at[part, k - 1],
+            away_sent.at[part],
+            away_landed.at[part],
             {"energy": peer},
         )
 
@@ -178,21 +176,35 @@
         return remote(
             sigma_s.at[peer, :, columns],
             back_s.at[me, :, columns],
-            back_sent.at[q, k - 1],
-            back_landed.at[q, k - 1],
+            back_sent.at[q],
+            back_landed.at[q],
             {"energy": peer},
         )
 
     def keep(part):
         at, columns = piece(part)
         return pltpu.make_async_copy(
-            mixed_s.at[me, at, :, columns], got_s.at[me, at, :, columns], own_away.at[part]
+            mixed_s.at[me, at, :, columns], got_s.at[me, at, :, columns], away_landed.at[part]
         )
 
     def keep_back(q):
         columns = pl.ds(q * pack * width, pack * width)
         return pltpu.make_async_copy(
-            sigma_s.at[me, :, columns], back_s.at[me, :, columns], own_back.at[q]
+            sigma_s.at[me, :, columns], back_s.at[me, :, columns], back_landed.at[q]
+        )
+
+    def all_away(part, count, sem):
+        at, columns = piece(part)
+        some = pl.ds(0, count)
+        return pltpu.make_async_copy(
+            mixed_s.at[some, at, :, columns], got_s.at[some, at, :, columns], sem.at[part]
+        )
+
+    def all_back(q, count, sem):
+        columns = pl.ds(q * pack * width, pack * width)
+        some = pl.ds(0, count)
+        return pltpu.make_async_copy(
+            sigma_s.at[some, :, columns], back_s.at[some, :, columns], sem.at[q]
         )
 
     def for_peers(action):
@@ -363,8 +375,7 @@
     for q in range(quads):
         for part in range(parts):
             if q == (early if part == 2 else 0):
-                for_peers(lambda k: away(part, k).wait_recv())
-                keep(part).wait()
+                all_away(part, owners, away_landed).wait()
         packed = got_s[:, :, :, q * width : (q + 1) * width].astype(F32)
         packed = packed.reshape(points * pack, width).astype(BF16)
         for r in range(pack):
@@ -386,8 +397,7 @@
 
     unmix = unmix_s[...]
     for q in range(quads):
-        for_peers(lambda k: back(q, k).wait_recv())
-        keep_back(q).wait()
+        all_back(q, owners, back_landed).wait()
         for r in range(q * pack, (q + 1) * pack):
             values = back_s[:, :, r * width : (r + 1) * width].astype(F32)
             values = values.reshape(points, width).astype(BF16)
@@ -395,9 +405,9 @@
     for b in range(batches):
         share_map(b).wait_send()
     for part in range(parts):
-        for_peers(lambda k: away(part, k).wait_send())
+        all_away(part, owners - 1, away_sent).wait()
     for q in range(quads):
-        for_peers(lambda k: back(q, k).wait_send())
+        all_back(q, owners - 1, back_sent).wait()
 
 
 def restore_kernel(slots_ref, place_ref, out_ref, result_s, out_sem):
@@ -405,16 +415,13 @@
     share, points, _ = slots_ref.shape
     owners = points // here
     place = place_ref[...]
-    outs = []
     for e in range(here):
         at = slice(e * owners, (e + 1) * owners)
         ordered = jnp.concatenate([slots_ref[r, at, :] for r in range(share)], axis=0)
         result_s[e] = dot(place, ordered)
-        out = pltpu.make_async_copy(result_s.at[e], out_ref.at[e], out_sem.at[e])
+        out = pltpu.make_async_copy(result_s.at[e], out_ref.at[e], out_sem.at[0])
         out.start()
-        outs.append(out)
-    for out in outs:
-        out.wait()
+    pltpu.make_async_copy(result_s, out_ref, out_sem.at[0]).wait()
 
 
 def on_device(owners, green0, coupling, pattern, broaden, screened, order):
@@ -458,7 +465,6 @@
     dma = pltpu.SemaphoreType.DMA
     cell = (here, 2 * size, size)
     packed = (owners, batches, 8, quads * width)
-    peers = owners - 1
     vmem = pl.BlockSpec(memory_space=pltpu.VMEM)
     slots, place = pl.pallas_call(
         functools.partial(fused_kernel, owners, pack, 1.0 / (points * math.sqrt(points))),
@@ -496,13 +502,11 @@
             dma((batches,)),
             dma((batches,)),
             dma((batches,)),
-            dma((3, peers)),
-            dma((3, peers)),
-            dma((quads, peers)),
-            dma((quads, peers)),
+            dma((3,)),
             dma((3,)),
             dma((quads,)),
-            pltpu.SemaphoreType.REGULAR((owners.bit_length(),)),
+            dma((quads,)),
+            pltpu.SemaphoreType.REGULAR((1 << (owners.bit_length() - 1) // 2,)),
         ],
         compiler_params=pltpu.CompilerParams(
             collective_id=0, has_side_effects=True, vmem_limit_bytes=44 << 20
@@ -525,7 +529,7 @@
         in_specs=[vmem, vmem],
         out_specs=anywhere,
         out_shape=jax.ShapeDtypeStruct((here, size, width), F32),
-        scratch_shapes=[pltpu.VMEM((here, size, width), F32), dma((here,))],
+        scratch_shapes=[pltpu.VMEM((here, size, width), F32), dma((1,))],
         compiler_params=pltpu.CompilerParams(vmem_limit_bytes=16 << 20),
         name="restore",
     )(slots, place)

time: 64.2 us -> 61.9 us (0.964)
  Pallas kernels: 63.8 us -> 61.6 us
    pallas_call x1, Pallas kernels: 62.2 us -> 59.9 us  [on_device(): pl.pallas_call(functools.partial(fused_kernel, owners, pack, 1.0 / (point...]
where the time goes in v4:
time: 61.9 us; the launch traced here: 61.7 us
  Pallas kernels  61.6 us (100%)
    pallas_call x1, Pallas kernels, on_device(): pl.pallas_call(functools.partial(fused_kernel, owners, pack, 1.0 / (point...  59.9 us
    pallas_call x1, Pallas kernels, on_device(): pl.pallas_call(restore_kernel, in_specs=[vmem, vmem], out_specs=anywhere,...  1.61 us

profile of v4, /device:TPU:0, one launch (start us, length us, event | category | flops | bytes accessed | tf_op | source)
XLA Modules:
  0.0 61.7 jit_solution(1074562851692253941)
XLA Ops:
  0.0 59.9 %fused.1 = (bf16[12,128,384]{2,1,0:T(8,128)(2,1)S(1)}, bf16[192,192]{1,0:T(8,128)(2,1)S(1)}) custom-call(s32[4,4]{1,0:T(4,128)} %bitcast.13, bf16[192,192]{1,0:T(8,128)(2,1)} %bitcast.12, bf16[8,384,192]{2,1,0:T(8,128)(2,1)} %bitcast.10, bf16[8,192,192]{2,1,0:T(8,128)(2,1)} %bitcast.11, s32[1,192]{1,0:T(1,128)} %bitcast.14, ...), custom_call_target="tpu_custom_call" | custom-call | tf_op jit(solution)/shard_map/fused/pallas_call | solution.py:469
  60.0 1.6 %restore.1 = f32[8,192,384]{2,1,0:T(8,128)} custom-call(bf16[12,128,384]{2,1,0:T(8,128)(2,1)S(1)} %get-tuple-element.7.slots_ref, bf16[192,192]{1,0:T(8,128)(2,1)S(1)} %get-tuple-element.8.place_ref), custom_call_target="tpu_custom_call" | custom-call | tf_op jit(solution)/shard_map/restore/pallas_call | solution.py:527

commit v5 on v4

--- a/solution.py
+++ b/solution.py
@@ -150,7 +150,7 @@
 
     def share_map(b):
         at = pl.ds(b * many, many)
-        return remote(send_s.at[at], map_s.at[at], map_sent.at[b], map_landed.at[b], {"space": 1 - cell})
+        return remote(send_s.at[at], map_s.at[at], map_sent.at[0], map_landed.at[b], {"space": 1 - cell})
 
     def piece(part):
         if part == 0:
@@ -165,7 +165,7 @@
         return remote(
             mixed_s.at[peer, at, :, columns],
             got_s.at[me, at, :, columns],
-            away_sent.at[part],
+            away_sent.at[0],
             away_landed.at[part],
             {"energy": peer},
         )
@@ -176,7 +176,7 @@
         return remote(
             sigma_s.at[peer, :, columns],
             back_s.at[me, :, columns],
-            back_sent.at[q],
+            back_sent.at[0],
             back_landed.at[q],
             {"energy": peer},
         )
@@ -193,18 +193,16 @@
             sigma_s.at[me, :, columns], back_s.at[me, :, columns], back_landed.at[q]
         )
 
-    def all_away(part, count, sem):
+    def all_away(part):
         at, columns = piece(part)
-        some = pl.ds(0, count)
         return pltpu.make_async_copy(
-            mixed_s.at[some, at, :, columns], got_s.at[some, at, :, columns], sem.at[part]
-        )
-
-    def all_back(q, count, sem):
+            mixed_s.at[:, at, :, columns], got_s.at[:, at, :, columns], away_landed.at[part]
+        )
+
+    def all_back(q):
         columns = pl.ds(q * pack * width, pack * width)
-        some = pl.ds(0, count)
         return pltpu.make_async_copy(
-            sigma_s.at[some, :, columns], back_s.at[some, :, columns], sem.at[q]
+            sigma_s.at[:, :, columns], back_s.at[:, :, columns], back_landed.at[q]
         )
 
     def for_peers(action):
@@ -289,9 +287,17 @@
             for e, f in zip(batch, flipped):
                 send_s[e] = dot(f, couple).astype(BF16)
                 other_s[e] = f
-            for e, g in zip(batch, green):
-                mult_s[e] = dot(g, couple).astype(BF16)
-                base_s[e] = g.astype(F32)
+
+    def rest(b):
+        batch = [b * many + i for i in range(many)]
+
+        @pl.when(cell == 1)
+        def _():
+            couple = couple_s[...]
+            for e in batch:
+                green = green_s[e]
+                mult_s[e] = dot(green, couple).astype(BF16)
+                base_s[e] = green.astype(F32)
 
     def lesser(b):
         batch = [b * many + i for i in range(many)]
@@ -324,6 +330,7 @@
     share_map(0).start()
     for d in range(1, low):
         say_ready(d)
+    rest(0)
     for b in range(2, batches):
         load_green(b).start()
     for each in (screened_load, table_load, turn_load, unmix_load):
@@ -331,6 +338,7 @@
     if batches > 1:
         born(1)
         share_map(1).start()
+        rest(1)
     order_load.wait()
     sort_load.wait()
     ids = lax.broadcasted_iota(jnp.int32, (size, size), 0)
@@ -349,6 +357,7 @@
         if b + 2 < batches:
             born(b + 2)
             share_map(b + 2).start()
+            rest(b + 2)
     for part in range(1, parts):
         for_peers(lambda k: away(part, k).start())
         keep(part).start()
@@ -375,7 +384,7 @@
     for q in range(quads):
         for part in range(parts):
             if q == (early if part == 2 else 0):
-                all_away(part, owners, away_landed).wait()
+                all_away(part).wait()
         packed = got_s[:, :, :, q * width : (q + 1) * width].astype(F32)
         packed = packed.reshape(points * pack, width).astype(BF16)
         for r in range(pack):
@@ -397,17 +406,15 @@
 
     unmix = unmix_s[...]
     for q in range(quads):
-        all_back(q, owners, back_landed).wait()
+        all_back(q).wait()
         for r in range(q * pack, (q + 1) * pack):
             values = back_s[:, :, r * width : (r + 1) * width].astype(F32)
             values = values.reshape(points, width).astype(BF16)
             slots_s[r] = dot(unmix, values).astype(BF16)
-    for b in range(batches):
-        share_map(b).wait_send()
-    for part in range(parts):
-        all_away(part, owners - 1, away_sent).wait()
-    for q in range(quads):
-        all_back(q, owners - 1, back_sent).wait()
+    others = pl.ds(0, owners - 1)
+    pltpu.make_async_copy(send_s, map_s, map_sent.at[0]).wait()
+    pltpu.make_async_copy(mixed_s.at[others], got_s.at[others], away_sent.at[0]).wait()
+    pltpu.make_async_copy(sigma_s.at[others], back_s.at[others], back_sent.at[0]).wait()
 
 
 def restore_kernel(slots_ref, place_ref, out_ref, result_s, out_sem):
@@ -500,11 +507,11 @@
             pltpu.VMEM((owners, here, flat), BF16),
             dma((9,)),
             dma((batches,)),
+            dma((1,)),
             dma((batches,)),
-            dma((batches,)),
+            dma((1,)),
             dma((3,)),
-            dma((3,)),
-            dma((quads,)),
+            dma((1,)),
             dma((quads,)),
             pltpu.SemaphoreType.REGULAR((1 << (owners.bit_length() - 1) // 2,)),
         ],

time: 61.9 us -> 61.7 us (level)
  no operation moved by 1% of the time
where the time goes in v5:
time: 61.7 us; the launch traced here: 61.5 us
  Pallas kernels  61.3 us (99%)
    pallas_call x1, Pallas kernels, on_device(): pl.pallas_call(functools.partial(fused_kernel, owners, pack, 1.0 / (point...  59.7 us
    pallas_call x1, Pallas kernels, on_device(): pl.pallas_call(restore_kernel, in_specs=[vmem, vmem], out_specs=anywhere,...  1.61 us

profile of v5, /device:TPU:0, one launch (start us, length us, event | category | flops | bytes accessed | tf_op | source)
XLA Modules:
  0.0 61.5 jit_solution(471283550679732067)
XLA Ops:
  0.0 59.7 %fused.1 = (bf16[12,128,384]{2,1,0:T(8,128)(2,1)S(1)}, bf16[192,192]{1,0:T(8,128)(2,1)S(1)}) custom-call(s32[4,4]{1,0:T(4,128)} %bitcast.13, bf16[192,192]{1,0:T(8,128)(2,1)} %bitcast.12, bf16[8,384,192]{2,1,0:T(8,128)(2,1)} %bitcast.10, bf16[8,192,192]{2,1,0:T(8,128)(2,1)} %bitcast.11, s32[1,192]{1,0:T(1,128)} %bitcast.14, ...), custom_call_target="tpu_custom_call" | custom-call | tf_op jit(solution)/shard_map/fused/pallas_call | solution.py:476
  59.7 1.6 %restore.1 = f32[8,192,384]{2,1,0:T(8,128)} custom-call(bf16[12,128,384]{2,1,0:T(8,128)(2,1)S(1)} %get-tuple-element.7.slots_ref, bf16[192,192]{1,0:T(8,128)(2,1)S(1)} %get-tuple-element.8.place_ref), custom_call_target="tpu_custom_call" | custom-call | tf_op jit(solution)/shard_map/restore/pallas_call | solution.py:534

commit v6 on v5

--- a/solution.py
+++ b/solution.py
@@ -170,9 +170,13 @@
             {"energy": peer},
         )
 
+    def back_columns(g):
+        count = 1 if g == 0 else quads - 1
+        return pl.ds(g * pack * width, count * pack * width)
+
     def back(q, k):
         peer = peer_of(k)
-        columns = pl.ds(q * pack * width, pack * width)
+        columns = back_columns(q)
         return remote(
             sigma_s.at[peer, :, columns],
             back_s.at[me, :, columns],
@@ -188,7 +192,7 @@
         )
 
     def keep_back(q):
-        columns = pl.ds(q * pack * width, pack * width)
+        columns = back_columns(q)
         return pltpu.make_async_copy(
             sigma_s.at[me, :, columns], back_s.at[me, :, columns], back_landed.at[q]
         )
@@ -200,7 +204,7 @@
         )
 
     def all_back(q):
-        columns = pl.ds(q * pack * width, pack * width)
+        columns = back_columns(q)
         return pltpu.make_async_copy(
             sigma_s.at[:, :, columns], back_s.at[:, :, columns], back_landed.at[q]
         )
@@ -401,12 +405,15 @@
             product = spectrum * kernel_re + times_i(spectrum) * kernel_im
             found = transform(table, times_i(product), product)
             sigma_s[:, :, at] = found.reshape(owners, here, width).astype(BF16)
-        for_peers(lambda k: back(q, k).start())
-        keep_back(q).start()
+        if q in (0, quads - 1):
+            group = min(q, 1)
+            for_peers(lambda k: back(group, k).start())
+            keep_back(group).start()
 
     unmix = unmix_s[...]
     for q in range(quads):
-        all_back(q).wait()
+        if q < 2:
+            all_back(q).wait()
         for r in range(q * pack, (q + 1) * pack):
             values = back_s[:, :, r * width : (r + 1) * width].astype(F32)
             values = values.reshape(points, width).astype(BF16)

time: 61.7 us -> 62.8 us (1.018)
  the two profiles are of different devices: /device:TPU:0 before, /device:TPU:28 now
where the time goes in v6:
time: 62.8 us; the launch traced here: 62.7 us
  Pallas kernels  62.5 us (100%)
    pallas_call x1, Pallas kernels, on_device(): pl.pallas_call(functools.partial(fused_kernel, owners, pack, 1.0 / (point...  60.9 us
    pallas_call x1, Pallas kernels, on_device(): pl.pallas_call(restore_kernel, in_specs=[vmem, vmem], out_specs=anywhere,...  1.61 us

profile of v6, /device:TPU:28, one launch (start us, length us, event | category | flops | bytes accessed | tf_op | source)
XLA Modules:
  0.0 62.7 jit_solution(3066552450178336211)
XLA Ops:
  0.0 60.9 %fused.1 = (bf16[12,128,384]{2,1,0:T(8,128)(2,1)S(1)}, bf16[192,192]{1,0:T(8,128)(2,1)S(1)}) custom-call(s32[4,4]{1,0:T(4,128)} %bitcast.13, bf16[192,192]{1,0:T(8,128)(2,1)} %bitcast.12, bf16[8,384,192]{2,1,0:T(8,128)(2,1)} %bitcast.10, bf16[8,192,192]{2,1,0:T(8,128)(2,1)} %bitcast.11, s32[1,192]{1,0:T(1,128)} %bitcast.14, ...), custom_call_target="tpu_custom_call" | custom-call | tf_op jit(solution)/shard_map/fused/pallas_call | solution.py:483
  60.9 1.6 %restore.1 = f32[8,192,384]{2,1,0:T(8,128)} custom-call(bf16[12,128,384]{2,1,0:T(8,128)(2,1)S(1)} %get-tuple-element.7.slots_ref, bf16[192,192]{1,0:T(8,128)(2,1)S(1)} %get-tuple-element.8.place_ref), custom_call_target="tpu_custom_call" | custom-call | tf_op jit(solution)/shard_map/restore/pallas_call | solution.py:541
